TPU v7x, 128 devices: a whole 4x4x4 slice. The times are simulated.
128 devices in a mesh: dp: 8 (over y, z_lo), mp: 16 (over x, z_hi, core).
Axes of the slice: x: 4, y: 4, z: 4 (z_hi: 2, z_lo: 2; z = z_hi * 2 + z_lo), core: 2. Of those that a mesh axis runs over, the one named last changes fastest.
Arguments:
- tokens: bfloat16 [8192, 8192], P(('dp', 'mp')), may hold values from -6 to 6
- row_counts: int32 [8, 16], replicated, may hold values from 8 to 64, as said below
- gate_blocks: bfloat16 [64, 16, 128, 256], P('mp'), may hold values from -0.125 to 0.125
- gate_index: int32 [64, 16], P('mp'), may hold values from 0 to 63, as said below
- up_blocks: bfloat16 [64, 16, 128, 256], P('mp'), may hold values from -0.125 to 0.125
- up_index: int32 [64, 16], P('mp'), may hold values from 0 to 63, as said below
- down_blocks: bfloat16 [64, 16, 256, 128], P('mp'), may hold values from -0.09375 to 0.09375
- down_index: int32 [64, 16], P('mp'), may hold values from 0 to 63, as said below
Outputs:
- layer_out: bfloat16 [8192, 8192], P(('dp', 'mp'))
Inputs may be any that keep to these rules, and one draw needn't show every extreme that they name: `row_counts`: every entry is a multiple of 8; the entries of one column (one mp index) add up to 32 times the number of dp indices, and every column holds one entry equal to 64. `gate_index`: each row holds 16 distinct block rows in increasing order. `up_index`: each row holds 16 distinct block rows in increasing order. `down_index`: each row holds 16 distinct block columns in increasing order.
All inputs are finite; a program needn't handle non-finite values.
Results may differ from a plain program's by a relative error of at most 0.013.
Values may be sent and summed in bfloat16 or wider, within the bound.
No kernel may reach another device: no remote copies, remote signals or barrier semaphores. Data moves between devices by JAX's collectives and lax.ppermute only.
A program may use at most 192 MiB of HBM per device.

v0:
```python
import jax
import jax.numpy as jnp
from jax import lax
from jax.sharding import PartitionSpec as P


def make_hidden(row_block, gate_blocks, gate_index, up_blocks, up_index):
    row_count = row_block.shape[0]
    block_width = gate_blocks.shape[2]
    split_rows = row_block.reshape(row_count, -1, block_width)
    gate_input = jnp.take(split_rows, gate_index, axis=1)
    up_input = jnp.take(split_rows, up_index, axis=1)
    gate_value = jnp.einsum(
        "rjkc,jkcn->rjn", gate_input, gate_blocks, preferred_element_type=jnp.float32
    )
    up_value = jnp.einsum("rjkc,jkcn->rjn", up_input, up_blocks, preferred_element_type=jnp.float32)
    hidden = (jax.nn.silu(gate_value) * up_value).astype(jnp.bfloat16)
    return hidden.reshape(row_count, -1)


def apply_down(hidden_rows, down_blocks, down_index, block_total):
    row_count = hidden_rows.shape[0]
    column_blocks = down_blocks.shape[0]
    nonzero_count = down_blocks.shape[1]
    block_width = down_blocks.shape[3]
    hidden_split = hidden_rows.reshape(row_count, column_blocks, down_blocks.shape[2])
    products = jnp.einsum(
        "rjn,jknc->rjkc", hidden_split, down_blocks, preferred_element_type=jnp.float32
    )
    flat_products = products.reshape(row_count, column_blocks * nonzero_count, block_width)
    placed = jnp.zeros((row_count, block_total, block_width), jnp.float32)
    placed = placed.at[:, down_index.reshape(-1)].add(flat_products)
    return placed.reshape(row_count, -1)


def body(tokens, row_counts, gate_blocks, gate_index, up_blocks, up_index, down_blocks, down_index):
    own_dp = lax.axis_index("dp")
    own_mp = lax.axis_index("mp")
    rows_in = tokens.shape[0]
    model_width = tokens.shape[1]
    block_total = model_width // down_blocks.shape[3]
    hidden_all = make_hidden(
        lax.all_gather(tokens, "mp", axis=0, tiled=True),
        gate_blocks,
        gate_index,
        up_blocks,
        up_index,
    )
    summed = lax.psum_scatter(
        apply_down(hidden_all, down_blocks, down_index, block_total).astype(jnp.bfloat16),
        "mp",
        scatter_dimension=0,
        tiled=True,
    ).astype(jnp.float32)
    valid_rows = jnp.arange(rows_in, dtype=jnp.int32) < row_counts[own_dp, own_mp]
    return jnp.where(valid_rows[:, None], summed, 0.0).astype(jnp.bfloat16)


def solution(mesh):
    in_specs = (
        P(("dp", "mp"), None),
        P(),
        P("mp", None, None, None),
        P("mp", None),
        P("mp", None, None, None),
        P("mp", None),
        P("mp", None, None, None),
        P("mp", None),
    )
    out_specs = P(("dp", "mp"), None)
    return jax.shard_map(body, mesh=mesh, in_specs=in_specs, out_specs=out_specs, check_vma=False)
```

profile of v0, /device:TPU:0, one launch (start us, length us, event | category | flops | bytes accessed | tf_op | source)
XLA Modules:
  0.0 531.5 jit_solution(15970325136171968062)
XLA Ops:
  6.5 0.7 all-gather.2.cloned.1.call-update
  7.3 0.8 reshape.48
  8.1 0.7 compare_select_fusion
  8.8 0.7 compare_select_fusion.1
  9.6 0.7 compare_and_fusion
  10.3 0.7 compare_and_fusion.1
  11.0 111.0 %all-gather.2.cloned.1.call-done = bf16[1024,8192]{1,0:T(8,128)(2,1)} async-done(((bf16[64,8192]{1,0:T(8,128)(2,1)}), bf16[1024,8192]{1,0:T(8,128)(2,1)}) %all-gather.2.cloned.1.call-update) | async-done | bytes 16777232 | tf_op jit(solution)/shard_map/all_gather | solution.py:43
  122.0 22.4 %copy.22 = bf16[1024,8192]{0,1:T(8,128)(2,1)} copy(bf16[1024,8192]{1,0:T(8,128)(2,1)} %all-gather.2.cloned.1.call-done) | data formatting | bytes 33554432 | tf_op jit(solution)/shard_map/all_gather | solution.py:43
  144.4 22.4 %copy.23 = bf16[1024,64,128]{2,0,1:T(8,128)(2,1)} copy(bf16[1024,64,128]{0,2,1:T(8,128)(2,1)} %bitcast.53) | data formatting | bytes 33554432 | tf_op jit(solution)/shard_map/reshape | solution.py:10
  166.8 13.3 %gather_fusion.1 = bf16[64,1024,128]{2,1,0:T(8,128)(2,1)} fusion(bf16[1024,64,128]{2,0,1:T(8,128)(2,1)} %copy.23, s32[1024]{0:T(1024)S(1)} %pad_clamp_fusion), kind=kCustom, calls=%fused_computation.1.clone | custom fusion | bytes 33554688 | tf_op jit(solution)/shard_map/jit(_take)/gather | solution.py:12
  180.1 13.4 %gather_fusion = bf16[64,1024,128]{2,1,0:T(8,128)(2,1)} fusion(bf16[1024,64,128]{2,0,1:T(8,128)(2,1)} %copy.23, s32[1024]{0:T(1024)S(1)} %pad_clamp_fusion.1), kind=kCustom, calls=%fused_computation.clone | custom fusion | bytes 33554688 | tf_op jit(solution)/shard_map/jit(_take)/gather | solution.py:11
  193.5 10.8 %fusion = f32[4,1024,256,1]{2,1,3,0:T(8,128)} fusion(bf16[4,16,128,256]{3,2,1,0:T(8,128)(2,1)} %param.14, bf16[4,16,1024,128]{3,2,1,0:T(8,128)(2,1)} %bitcast.56, pred[4,16]{1,0:T(4,128)(4,1)S(1)} %compare_and_fusion), kind=kOutput, calls=%fused_computation.3 | convolution fusion | flops 4303355904 | bytes 25165888 | tf_op jit(solution)/shard_map/rjkc,jkcn->rjn/dot_general | solution.py:16
  204.3 2.5 copy-done
  206.7 8.6 %fusion.10 = bf16[1024,4,256]{2,0,1:T(8,128)(2,1)} fusion(f32[4,1024,256,1]{2,1,3,0:T(8,128)} %fusion, bf16[4,16,128,256]{3,2,1,0:T(8,128)(2,1)} %param.12, bf16[4,16,1024,128]{3,2,1,0:T(8,128)(2,1)S(1)} %bitcast.55, pred[4,16]{1,0:T(4,128)(4,1)S(1)} %compare_and_fusion.1), kind=kOutput, calls=%fused_computation.14 | convolution fusion | flops 4309647360 | bytes 27263040 | tf_op jit(solution)/shard_map/rjkc,jkcn->rjn/dot_general | solution.py:13
  215.3 18.4 %fusion.16 = f32[4,1024,16,128]{3,1,2,0:T(8,128)} fusion(bf16[4,16,256,128]{3,2,1,0:T(8,128)(2,1)} %param.16, bf16[1024,4,256]{2,0,1:T(8,128)(2,1)} %fusion.10), kind=kOutput, calls=%fused_computation.20 | convolution fusion | flops 4294967296 | bytes 39845888 | tf_op jit(solution)/shard_map/rjn,jknc->rjkc/dot_general | solution.py:27
  233.8 11.0 %broadcast_in_dim.27 = f32[1024,64,128]{2,0,1:T(8,128)} broadcast(f32[]{:T(128)} %constant.9.clone.1), dimensions={} | broadcast | bytes 33554436 | tf_op jit(solution)/shard_map/broadcast_in_dim | solution.py:31
  244.7 71.2 %scatter_fusion = f32[1024,64,128]{2,0,1:T(8,128)} fusion(f32[1024,64,128]{2,0,1:T(8,128)} %broadcast_in_dim.27, s32[64]{0:T(128)S(1)} %fusion.18, f32[64,1024,128]{2,1,0:T(8,128)} %bitcast.52), kind=kCustom, calls=%fused_computation.2 | custom fusion | flops 8388608 | bytes 100663552 | tf_op jit(solution)/shard_map/scatter-add | solution.py:32
  316.0 17.6 %convert_element_type.16 = bf16[1024,64,128]{2,0,1:T(8,128)(2,1)} convert(f32[1024,64,128]{2,0,1:T(8,128)} %scatter_fusion) | non-fusion elementwise | flops 8388608 | bytes 50331648 | tf_op jit(solution)/shard_map/convert_element_type | solution.py:50
  333.5 22.4 %copy.25 = bf16[1024,64,128]{0,2,1:T(8,128)(2,1)} copy(bf16[1024,64,128]{2,0,1:T(8,128)(2,1)} %convert_element_type.16) | data formatting | bytes 33554432 | tf_op jit(solution)/shard_map/convert_element_type | solution.py:50
  355.9 21.0 %copy.30 = bf16[1024,8192]{1,0:T(8,128)(2,1)} copy(bf16[1024,8192]{0,1:T(8,128)(2,1)} %bitcast.54) | data formatting | bytes 33554432
  377.0 1.3 dynamic_slice.3
  378.3 0.6 iota_compare_fusion
  378.9 143.3 %reduce-scatter.4.cloned.1.call-done = bf16[64,8192]{1,0:T(8,128)(2,1)} async-done(((bf16[1024,8192]{1,0:T(8,128)(2,1)}), bf16[64,8192]{1,0:T(8,128)(2,1)}) %reduce-scatter.4.cloned.1.call-update) | async-done | bytes 1048592 | tf_op jit(solution)/shard_map/reduce_scatter | solution.py:49
  522.2 2.4 select_convert_fusion
  (9 shorter events, 0.2 us)
Async XLA Ops:
  6.5 115.5 %all-gather.2.cloned.1.call-start = ((), (), s32[]{:S(2)}) async-start(), calls=%async_computation.1 | async-start | bytes 17825792 | tf_op jit(solution)/shard_map/all_gather | solution.py:43
  7.3 515.0 %reduce-scatter.4.cloned.1.call-start = ((), (), s32[]{:S(2)}) async-start(), calls=%async_computation.2 | async-start | bytes 17825792 | tf_op jit(solution)/shard_map/reduce_scatter | solution.py:49
  193.5 13.3 %copy-start = (bf16[64,1024,128]{2,1,0:T(8,128)(2,1)S(1)}, bf16[64,1024,128]{2,1,0:T(8,128)(2,1)}, u32[]{:S(2)}) copy-start(bf16[64,1024,128]{2,1,0:T(8,128)(2,1)} %gather_fusion) | copy-start | bytes 50331652
Sparse Core Ops, SparseCore 0:
  9.7 112.2 all-gather.1
  377.1 145.0 reduce-scatter.3
where the time goes:
time: 534 us; the launch traced here: 531 us
  waiting for transfers between devices  255 us (48%)
  local copies, waits for them, and re-layouts  131 us (25%)
  other arithmetic  94.6 us (18%)
  matrix products  37.8 us (7%)
  between operations  13.4 us (3%)
    reduce_scatter x1, waiting for transfers between devices, body(): lax.psum_scatter(apply_down(hidden_all, down_blocks, down_index, block_to...  143 us
    all_gather x1, waiting for transfers between devices, body(): lax.all_gather(tokens, 'mp', axis=0, tiled=True)  111 us
    scatter-add x1, other arithmetic, apply_down(): placed = placed.at[:, down_index.reshape(-1)].add(flat_products)  71.2 us
    unnamed x3, local copies, waits for them, and re-layouts  23.5 us
    all_gather x1, local copies, waits for them, and re-layouts, body(): lax.all_gather(tokens, 'mp', axis=0, tiled=True)  22.4 us
    convert_element_type x1, local copies, waits for them, and re-layouts, body(): apply_down(hidden_all, down_blocks, down_index, block_total)  22.4 us
    reshape x1, local copies, waits for them, and re-layouts, make_hidden(): split_rows = row_block.reshape(row_count, -1, block_width)  22.4 us
    dot_general x1, matrix products, apply_down(): jnp.einsum('rjn,jknc->rjkc', hidden_split, down_blocks, preferred_element...  18.4 us
  transfers between devices with their start and end apart: 2, of which 2 were waited for; matrix products, arithmetic and copies ran while one was open for 1% of the time, Pallas kernels for 0%

commit v1 on v0

--- a/solution.py
+++ b/solution.py
@@ -2,6 +2,11 @@
 import jax.numpy as jnp
 from jax import lax
 from jax.sharding import PartitionSpec as P
+
+
+def gather_over(x, axis, d):
+    stack = jnp.stack([x] * lax.axis_size(axis))
+    return jnp.concatenate(lax.all_to_all(stack, axis, 0, 0), axis=d)
 
 
 def make_hidden(row_block, gate_blocks, gate_index, up_blocks, up_index):
@@ -40,11 +45,7 @@
     model_width = tokens.shape[1]
     block_total = model_width // down_blocks.shape[3]
     hidden_all = make_hidden(
-        lax.all_gather(tokens, "mp", axis=0, tiled=True),
-        gate_blocks,
-        gate_index,
-        up_blocks,
-        up_index,
+        gather_over(tokens, "mp", 0), gate_blocks, gate_index, up_blocks, up_index
     )
     summed = lax.psum_scatter(
         apply_down(hidden_all, down_blocks, down_index, block_total).astype(jnp.bfloat16),

time: 534 us -> 709 us (1.33)
  waiting for transfers between devices: 255 us -> 418 us
  starting transfers between devices: 0.04 us -> 8.06 us
    all_to_all x0 -> x1, waiting for transfers between devices: none -> 270 us  [gather_over(): return jnp.concatenate(lax.all_to_all(stack, axis, 0, 0), axis=d)]
    all_gather x1 -> x0, waiting for transfers between devices: 111 us -> none  [body(): lax.all_gather(tokens, 'mp', axis=0, tiled=True)]
    another operation x0 -> x2, local copies, waits for them, and re-layouts: none -> 42.8 us  [the longest x1 36 us: make_hidden(): split_rows = row_block.reshape(row_count, -1, block_width)]
    all_gather x1 -> x0, local copies, waits for them, and re-layouts: 22.4 us -> none  [body(): lax.all_gather(tokens, 'mp', axis=0, tiled=True)]
    reshape x1 -> x0, local copies, waits for them, and re-layouts: 22.4 us -> none  [make_hidden(): split_rows = row_block.reshape(row_count, -1, block_width)]
    unnamed x3 -> x10, local copies, waits for them, and re-layouts: 23.5 us -> 33.5 us
    all_to_all x0 -> x1, starting transfers between devices: none -> 8.02 us  [gather_over(): return jnp.concatenate(lax.all_to_all(stack, axis, 0, 0), axis=d)]
  transfers between devices with their start and end apart: 2 -> 2, of which waited for: 2 -> 2; matrix products, arithmetic and copies ran while one was open for 1% -> 0% of each run, Pallas kernels for 0% -> 0%
where the time goes in v1:
time: 709 us; the launch traced here: 707 us
  waiting for transfers between devices  418 us (59%)
  local copies, waits for them, and re-layouts  138 us (19%)
  other arithmetic  91.9 us (13%)
  matrix products  37.8 us (5%)
  between operations  13.5 us (2%)
  starting transfers between devices  8.06 us (1%)
    all_to_all x1, waiting for transfers between devices, gather_over(): return jnp.concatenate(lax.all_to_all(stack, axis, 0, 0), axis=d)  270 us
    reduce_scatter x1, waiting for transfers between devices, body(): lax.psum_scatter(apply_down(hidden_all, down_blocks, down_index, block_to...  148 us
    scatter-add x1, other arithmetic, apply_down(): placed = placed.at[:, down_index.reshape(-1)].add(flat_products)  71.3 us
    another operation x1, local copies, waits for them, and re-layouts, make_hidden(): split_rows = row_block.reshape(row_count, -1, block_width)  36 us
    unnamed x10, local copies, waits for them, and re-layouts  33.5 us
    convert_element_type x1, local copies, waits for them, and re-layouts, body(): apply_down(hidden_all, down_blocks, down_index, block_total)  22.4 us
    dot_general x1, matrix products, apply_down(): jnp.einsum('rjn,jknc->rjkc', hidden_split, down_blocks, preferred_element...  18.4 us
    convert_element_type x1, other arithmetic, body(): apply_down(hidden_all, down_blocks, down_index, block_total)  17.5 us
  transfers between devices with their start and end apart: 2, of which 2 were waited for; matrix products, arithmetic and copies ran while one was open for 0% of the time, Pallas kernels for 0%

profile of v1, /device:TPU:0, one launch (start us, length us, event | category | flops | bytes accessed | tf_op | source)
XLA Modules:
  0.0 707.3 jit_solution(2983541110454539969)
XLA Ops:
  6.5 6.8 stack.2
  13.3 8.0 %all-to-all-start = ((bf16[16,64,8192]{2,1,0:T(8,128)(2,1)}), bf16[16,64,8192]{2,1,0:T(8,128)(2,1)}, u32[]{:S(2)}, u32[]{:S(2)}) async-start(bf16[16,64,8192]{2,1,0:T(8,128)(2,1)} %stack.2), calls=%async_computation | async-start | bytes 33554432 | tf_op jit(solution)/shard_map/all_to_all | solution.py:9
  21.4 0.0 reduce-scatter.4.cloned.1.call-start
  21.4 0.1 reshape.47
  21.5 0.1 reshape.81
  21.6 0.1 reshape.77
  21.7 269.9 %all-to-all-done = bf16[16,64,8192]{2,1,0:T(8,128)(2,1)} async-done(((bf16[16,64,8192]{2,1,0:T(8,128)(2,1)}), bf16[16,64,8192]{2,1,0:T(8,128)(2,1)}, u32[]{:S(2)}, u32[]{:S(2)}) %all-to-all-start) | async-done | bytes 16777248 | tf_op jit(solution)/shard_map/all_to_all | solution.py:9
  291.6 9.7 %copy.28 = bf16[128,8,64,128]{3,2,1,0:T(8,128)(2,1)S(1)} copy(bf16[128,8,64,128]{3,1,2,0:T(8,128)(2,1)} %bitcast.25) | data formatting | bytes 33554432
  301.3 36.0 %copy.19 = bf16[1024,64,128]{2,0,1:T(8,128)(2,1)} copy(bf16[1024,64,128]{2,1,0:T(8,128)(2,1)S(1)} %bitcast.55) | data formatting | bytes 33554432 | tf_op jit(solution)/shard_map/reshape;reshape | solution.py:15
  337.3 13.3 %gather_fusion.1 = bf16[64,1024,128]{2,1,0:T(8,128)(2,1)} fusion(bf16[1024,64,128]{2,0,1:T(8,128)(2,1)} %copy.19, s32[1024]{0:T(1024)S(1)} %pad_clamp_fusion), kind=kCustom, calls=%fused_computation.1.clone | custom fusion | bytes 33554688 | tf_op jit(solution)/shard_map/jit(_take)/gather | solution.py:17
  350.6 13.3 %gather_fusion = bf16[64,1024,128]{2,1,0:T(8,128)(2,1)} fusion(bf16[1024,64,128]{2,0,1:T(8,128)(2,1)} %copy.19, s32[1024]{0:T(1024)S(1)} %pad_clamp_fusion.1), kind=kCustom, calls=%fused_computation.clone | custom fusion | bytes 33554688 | tf_op jit(solution)/shard_map/jit(_take)/gather | solution.py:16
  363.9 10.8 %fusion = f32[4,1024,256,1]{2,1,3,0:T(8,128)} fusion(bf16[4,16,128,256]{3,2,1,0:T(8,128)(2,1)} %param.14, bf16[4,16,1024,128]{3,2,1,0:T(8,128)(2,1)} %bitcast.58, pred[4,16]{1,0:T(4,128)(4,1)S(1)} %compare_and_fusion), kind=kOutput, calls=%fused_computation.3 | convolution fusion | flops 4303355904 | bytes 25165888 | tf_op jit(solution)/shard_map/rjkc,jkcn->rjn/dot_general | solution.py:21
  374.7 2.4 copy-done
  377.2 8.6 %fusion.10 = bf16[1024,4,256]{2,0,1:T(8,128)(2,1)} fusion(f32[4,1024,256,1]{2,1,3,0:T(8,128)} %fusion, bf16[4,16,128,256]{3,2,1,0:T(8,128)(2,1)} %param.12, bf16[4,16,1024,128]{3,2,1,0:T(8,128)(2,1)S(1)} %bitcast.57, pred[4,16]{1,0:T(4,128)(4,1)S(1)} %compare_and_fusion.1), kind=kOutput, calls=%fused_computation.14 | convolution fusion | flops 4309647360 | bytes 27263040 | tf_op jit(solution)/shard_map/rjkc,jkcn->rjn/dot_general | solution.py:18
  385.7 18.4 %fusion.16 = f32[4,1024,16,128]{3,1,2,0:T(8,128)} fusion(bf16[4,16,256,128]{3,2,1,0:T(8,128)(2,1)} %param.16, bf16[1024,4,256]{2,0,1:T(8,128)(2,1)} %fusion.10), kind=kOutput, calls=%fused_computation.20 | convolution fusion | flops 4294967296 | bytes 39845888 | tf_op jit(solution)/shard_map/rjn,jknc->rjkc/dot_general | solution.py:32
  404.1 11.0 %broadcast_in_dim.27 = f32[1024,64,128]{2,0,1:T(8,128)} broadcast(f32[]{:T(128)} %constant.9.clone.1), dimensions={} | broadcast | bytes 33554436 | tf_op jit(solution)/shard_map/broadcast_in_dim | solution.py:36
  415.1 71.3 %scatter_fusion = f32[1024,64,128]{2,0,1:T(8,128)} fusion(f32[1024,64,128]{2,0,1:T(8,128)} %broadcast_in_dim.27, s32[64]{0:T(128)S(1)} %fusion.18, f32[64,1024,128]{2,1,0:T(8,128)} %bitcast.54), kind=kCustom, calls=%fused_computation.2 | custom fusion | flops 8388608 | bytes 100663552 | tf_op jit(solution)/shard_map/scatter-add | solution.py:37
  486.4 17.5 %convert_element_type.16 = bf16[1024,64,128]{2,0,1:T(8,128)(2,1)} convert(f32[1024,64,128]{2,0,1:T(8,128)} %scatter_fusion) | non-fusion elementwise | flops 8388608 | bytes 50331648 | tf_op jit(solution)/shard_map/convert_element_type | solution.py:51
  503.9 22.4 %copy.21 = bf16[1024,64,128]{0,2,1:T(8,128)(2,1)} copy(bf16[1024,64,128]{2,0,1:T(8,128)(2,1)} %convert_element_type.16) | data formatting | bytes 33554432 | tf_op jit(solution)/shard_map/convert_element_type | solution.py:51
  526.3 21.4 %copy.26 = bf16[1024,8192]{1,0:T(8,128)(2,1)} copy(bf16[1024,8192]{0,1:T(8,128)(2,1)} %bitcast.56) | data formatting | bytes 33554432
  547.7 1.3 dynamic_slice.3
  549.0 0.6 iota_compare_fusion
  549.7 148.4 %reduce-scatter.4.cloned.1.call-done = bf16[64,8192]{1,0:T(8,128)(2,1)} async-done(((bf16[1024,8192]{1,0:T(8,128)(2,1)}), bf16[64,8192]{1,0:T(8,128)(2,1)}) %reduce-scatter.4.cloned.1.call-update) | async-done | bytes 1048592 | tf_op jit(solution)/shard_map/reduce_scatter | solution.py:50
  698.1 2.4 select_convert_fusion
  (15 shorter events, 0.1 us)
Async XLA Ops:
  13.3 8.1 %copy-start.3 = (s32[4,16]{1,0:T(4,128)S(1)}, s32[4,16]{1,0:T(4,128)}, u32[]{:S(2)}) copy-start(s32[4,16]{1,0:T(4,128)} %param.17) | copy-start | bytes 772
  13.3 8.2 %copy-start.1 = (s32[4,16]{1,0:T(4,128)S(1)}, s32[4,16]{1,0:T(4,128)}, u32[]{:S(2)}) copy-start(s32[4,16]{1,0:T(4,128)} %param.15) | copy-start | bytes 772
  13.3 8.3 %copy-start.2 = (s32[4,16]{1,0:T(4,128)S(1)}, s32[4,16]{1,0:T(4,128)}, u32[]{:S(2)}) copy-start(s32[4,16]{1,0:T(4,128)} %param.13) | copy-start | bytes 772
  13.3 278.3 %all-to-all-start = ((bf16[16,64,8192]{2,1,0:T(8,128)(2,1)}), bf16[16,64,8192]{2,1,0:T(8,128)(2,1)}, u32[]{:S(2)}, u32[]{:S(2)}) async-start(bf16[16,64,8192]{2,1,0:T(8,128)(2,1)} %stack.2), calls=%async_computation | async-start | bytes 33554432 | tf_op jit(solution)/shard_map/all_to_all | solution.py:9
  21.4 676.7 %reduce-scatter.4.cloned.1.call-start = ((), (), s32[]{:S(2)}) async-start(), calls=%async_computation.2 | async-start | bytes 17825792 | tf_op jit(solution)/shard_map/reduce_scatter | solution.py:50
  363.9 13.3 %copy-start = (bf16[64,1024,128]{2,1,0:T(8,128)(2,1)S(1)}, bf16[64,1024,128]{2,1,0:T(8,128)(2,1)}, u32[]{:S(2)}) copy-start(bf16[64,1024,128]{2,1,0:T(8,128)(2,1)} %gather_fusion) | copy-start | bytes 50331652
Sparse Core Ops, SparseCore 0:
  547.8 150.1 reduce-scatter.3
